TPU v7x, 128 devices: a whole 4x4x4 slice. The times are simulated.
128 devices in a mesh: tok: 8 (over x, z_hi), feat: 16 (over y, z_lo, core).
Axes of the slice: x: 4, y: 4, z: 4 (z_hi: 2, z_lo: 2; z = z_hi * 2 + z_lo), core: 2. Of those that a mesh axis runs over, the one named last changes fastest.
Arguments:
- resid: bfloat16 [2048, 8192], P(None, ('tok', 'feat')), may hold values from -6 to 6
- resid_grad: bfloat16 [2048, 8192], P(None, ('tok', 'feat')), may hold values from -6 to 6
- active: int32 [16, 20], P('tok'), may hold values from 0 to 79, all different within a row
- w_enc: bfloat16 [8192, 10240], P(None, 'feat'), may hold values from -0.0625 to 0.0625
- b_enc: float32 [10240], P('feat'), may hold values from -3 to 3
- w_dec: bfloat16 [10240, 8192], P('feat'), may hold values from -0.25 to 0.25
- b_dec: float32 [8192], P('feat'), may hold values from -3 to 3
Outputs:
- feature_attr: float32 [2048, 10240], P('tok', 'feat')
- error: float32 [2048, 8192], P('tok', 'feat')
- error_attr: float32 [2048], P('tok')
Inputs may be any that keep to these rules, and one draw needn't show every extreme that they name: `active`: each row lists 20 different feature blocks; every block is listed by some tile.
All inputs are finite; a program needn't handle non-finite values.
Results may differ from a plain program's by a relative error of at most 0.012.
Values may be sent and summed in bfloat16 or wider, within the bound.
A program may use at most 128 MiB of HBM per device.

v0:
```python
import jax
import jax.numpy as jnp
from jax import lax
from jax.sharding import PartitionSpec as P

BLOCK = 128
TILE = 128


def per_device(resid, resid_grad, active, w_enc, b_enc, w_dec, b_dec):
    n_feat = lax.axis_size("feat")
    width = resid.shape[1]
    cols_x, cols_g = (
        lax.all_gather(resid[:, None, :], "feat", axis=1, tiled=True),
        lax.all_gather(resid_grad[:, None, :], "feat", axis=1, tiled=True),
    )
    total = cols_x.shape[0]
    cols_x = cols_x.reshape(total, n_feat * width)
    cols_g = cols_g.reshape(total, n_feat * width)
    rows_x, rows_g = (
        lax.all_to_all(cols_x, "tok", split_axis=0, concat_axis=1, tiled=True),
        lax.all_to_all(cols_g, "tok", split_axis=0, concat_axis=1, tiled=True),
    )
    tok_rows = rows_x.shape[0]
    feat_dev = w_enc.shape[1]
    blocks = feat_dev // BLOCK
    tiles_dev = active.shape[0]
    block_ids = lax.axis_index("feat") * blocks + jnp.arange(blocks, dtype=jnp.int32)
    hits = jnp.any(active[:, :, None] == block_ids[None, None, :], axis=1).astype(jnp.float32)
    pre = jnp.dot(rows_x, w_enc, preferred_element_type=jnp.float32) + b_enc
    shaped = jnp.maximum(pre, 0.0).reshape(tiles_dev, TILE, blocks, BLOCK) * hits[:, None, :, None]
    acts = shaped.reshape(tok_rows, feat_dev).astype(jnp.bfloat16)
    partial_recon = jnp.dot(acts, w_dec, preferred_element_type=jnp.float32)
    recon_share = lax.psum_scatter(
        partial_recon.astype(jnp.bfloat16), "feat", scatter_dimension=1, tiled=True
    ).astype(jnp.float32)
    share = recon_share.shape[1]
    start = lax.axis_index("feat") * share
    own_x = lax.dynamic_slice_in_dim(rows_x, start, share, 1)
    own_g = lax.dynamic_slice_in_dim(rows_g, start, share, 1)
    recon = recon_share + b_dec
    error = own_x.astype(jnp.float32) - recon
    local_terms = jnp.sum(error * own_g.astype(jnp.float32), axis=1)
    error_attr = lax.psum(local_terms, "feat")
    proj = lax.dot_general(
        rows_g, w_dec, (((1,), (1,)), ((), ())), preferred_element_type=jnp.float32
    )
    feature_attr = acts.astype(jnp.float32) * proj
    return (feature_attr, error, error_attr)


def solution(mesh):
    placed = (
        P(None, ("tok", "feat")),
        P(None, ("tok", "feat")),
        P("tok", None),
        P(None, "feat"),
        P("feat"),
        P("feat", None),
        P("feat"),
    )
    return jax.shard_map(
        per_device,
        mesh=mesh,
        in_specs=placed,
        out_specs=(P("tok", "feat"), P("tok", "feat"), P("tok")),
        check_vma=False,
    )
```

profile of v0, /device:TPU:0, one launch (start us, length us, event | category | flops | bytes accessed | tf_op | source)
XLA Modules:
  0.0 284.6 jit_solution(3607693962824944712)
XLA Ops:
  7.2 0.0 all-gather.5.cloned.1.call-start
  7.2 0.7 all-gather.5.cloned.1.call-update
  7.9 0.0 all-gather.7.cloned.1.call-start
  7.9 0.7 all-gather.7.cloned.1.call-update
  8.6 40.8 %all-gather.5.cloned.1.call-done = bf16[2048,1024]{0,1:T(8,128)(2,1)} async-done(((bf16[2048,64]{0,1:T(8,128)(2,1)}), bf16[2048,1024]{0,1:T(8,128)(2,1)}) %all-gather.5.cloned.1.call-update) | async-done | bytes 4194320 | tf_op jit(solution)/shard_map/all_gather | solution.py:14
  49.5 6.4 %copy.20 = bf16[2048,1024]{1,0:T(8,128)(2,1)} copy(bf16[2048,1024]{0,1:T(8,128)(2,1)} %all-gather.5.cloned.1.call-done) | data formatting | bytes 8388608 | tf_op jit(solution)/shard_map/all_gather | solution.py:14
  55.8 0.0 copy-start.3
  55.8 6.6 %all-to-all-start = ((bf16[8,256,1024]{2,1,0:T(8,128)(2,1)}), bf16[8,256,1024]{2,1,0:T(8,128)(2,1)}, u32[]{:S(2)}, u32[]{:S(2)}) async-start(bf16[8,256,1024]{2,1,0:T(8,128)(2,1)} %bitcast.21), calls=%async_computation | async-start | bytes 8388608 | tf_op jit(solution)/shard_map/all_to_all | solution.py:21
  62.5 0.0 reduce-scatter.2.cloned.1.call-start
  62.5 0.0 copy-done.3
  62.5 0.2 compare_reduce_fusion
  62.7 0.1 copy.22
  62.8 0.2 mul.24
  63.1 0.2 copy.23
  63.4 59.7 %all-to-all-done = bf16[8,256,1024]{2,1,0:T(8,128)(2,1)} async-done(((bf16[8,256,1024]{2,1,0:T(8,128)(2,1)}), bf16[8,256,1024]{2,1,0:T(8,128)(2,1)}, u32[]{:S(2)}, u32[]{:S(2)}) %all-to-all-start) | async-done | bytes 4194336 | tf_op jit(solution)/shard_map/all_to_all | solution.py:21
  123.1 0.0 copy-start.4
  123.1 0.0 slice-start
  123.1 2.9 %copy.26 = bf16[8,32,8,1024]{3,2,0,1:T(8,128)(2,1)S(1)} copy(bf16[8,32,8,1024]{3,2,1,0:T(8,128)(2,1)} %bitcast.4) | data formatting | bytes 8388608 | tf_op jit(solution)/shard_map/all_to_all | solution.py:21
  126.0 0.0 copy-start
  126.0 2.0 copy-done
  127.9 0.0 copy-done.4
  127.9 0.0 slice-start.1
  127.9 0.0 slice-start.2
  127.9 6.5 %fusion.2 = bf16[256,640]{1,0:T(8,128)(2,1)S(1)} fusion(f32[256,640]{1,0:T(8,128)S(1)} %copy.23, bf16[256,8192]{1,0:T(8,128)(2,1)S(1)} %bitcast.23, bf16[8192,640]{1,0:T(8,128)(2,1)} %param.10, f32[640]{0:T(1024)S(1)} %copy-done.4), kind=kOutput, calls=%fused_computation.5 | convolution fusion | flops 2685009920 | bytes 15665664 | tf_op jit(solution)/shard_map/dot_general | solution.py:30
  134.4 0.0 slice-done
  134.4 0.0 slice-done.1
  134.4 0.0 slice-done.2
  134.4 4.9 %convolution_convert_fusion = bf16[256,8192]{1,0:T(8,128)(2,1)} fusion(bf16[256,640]{1,0:T(8,128)(2,1)S(1)} %fusion.2, bf16[640,8192]{1,0:T(8,128)(2,1)S(1)} %bitcast.30), kind=kOutput, calls=%fused_computation | convolution fusion | flops 2686451712 | bytes 15007744 | tf_op jit(solution)/shard_map/dot_general | solution.py:33
  139.4 0.0 reduce-scatter.2.cloned.1.call-update
  139.4 0.0 all-gather.7.cloned.1.call-done
  139.4 6.4 %copy.24 = bf16[2048,1024]{1,0:T(8,128)(2,1)} copy(bf16[2048,1024]{0,1:T(8,128)(2,1)} %all-gather.7.cloned.1.call-done) | data formatting | bytes 8388608 | tf_op jit(solution)/shard_map/all_gather | solution.py:15
  145.8 4.8 %all-to-all-start.1 = ((bf16[8,256,1024]{2,1,0:T(8,128)(2,1)}), bf16[8,256,1024]{2,1,0:T(8,128)(2,1)}, u32[]{:S(2)}, u32[]{:S(2)}) async-start(bf16[8,256,1024]{2,1,0:T(8,128)(2,1)} %bitcast.22), calls=%async_computation.1 | async-start | bytes 8388608 | tf_op jit(solution)/shard_map/all_to_all | solution.py:22
  150.6 61.9 %all-to-all-done.1 = bf16[8,256,1024]{2,1,0:T(8,128)(2,1)} async-done(((bf16[8,256,1024]{2,1,0:T(8,128)(2,1)}), bf16[8,256,1024]{2,1,0:T(8,128)(2,1)}, u32[]{:S(2)}, u32[]{:S(2)}) %all-to-all-start.1) | async-done | bytes 4194336 | tf_op jit(solution)/shard_map/all_to_all | solution.py:22
  212.5 2.7 copy.27
  215.2 0.0 copy-start.1
  215.2 1.9 copy-done.1
  217.1 0.0 copy-start.2
  217.1 7.1 %convolution_multiply_fusion = f32[256,640]{1,0:T(8,128)} fusion(bf16[256,8192]{1,0:T(8,128)(2,1)S(1)} %bitcast.25, bf16[640,8192]{1,0:T(8,128)(2,1)} %param.12, bf16[256,640]{1,0:T(8,128)(2,1)S(1)} %fusion.2), kind=kOutput, calls=%fused_computation.1 | convolution fusion | flops 2684682240 | bytes 15663104 | tf_op jit(solution)/shard_map/dot_general | solution.py:45
  224.2 22.1 %reduce-scatter.2.cloned.1.call-done = bf16[256,512]{1,0:T(8,128)(2,1)} async-done(((bf16[256,8192]{1,0:T(8,128)(2,1)}), bf16[256,512]{1,0:T(8,128)(2,1)}) %reduce-scatter.2.cloned.1.call-update) | async-done | bytes 262160 | tf_op jit(solution)/shard_map/reduce_scatter | solution.py:34
  246.3 0.0 copy-done.2
  246.3 2.0 multiply_reduce_fusion
  248.3 29.7 %psum.7 = f32[256]{0:T(256)} all-reduce(f32[256]{0:T(256)S(1)} %get-tuple-element.3), channel_id=1, replica_groups=mesh['tok'=8,'feat'=16] {'feat'}, use_global_device_ids=true, to_apply=%region_3.0 | all-reduce | flops 256 | bytes 2048 | tf_op jit(solution)/shard_map/psum | solution.py:44
  (4 shorter events, 0.1 us)
Async XLA Ops:
  7.2 42.3 %all-gather.5.cloned.1.call-start = ((), (), s32[]{:S(2)}) async-start(), calls=%async_computation.4 | async-start | bytes 4456448 | tf_op jit(solution)/shard_map/all_gather | solution.py:14
  7.9 131.5 %all-gather.7.cloned.1.call-start = ((), (), s32[]{:S(2)}) async-start(), calls=%async_computation.5 | async-start | bytes 4456448 | tf_op jit(solution)/shard_map/all_gather | solution.py:15
  55.8 6.7 %copy-start.3 = (s32[2,20]{1,0:T(2,128)S(1)}, s32[2,20]{1,0:T(2,128)}, u32[]{:S(2)}) copy-start(s32[2,20]{1,0:T(2,128)} %param.9) | copy-start | bytes 484
  55.8 67.2 %all-to-all-start = ((bf16[8,256,1024]{2,1,0:T(8,128)(2,1)}), bf16[8,256,1024]{2,1,0:T(8,128)(2,1)}, u32[]{:S(2)}, u32[]{:S(2)}) async-start(bf16[8,256,1024]{2,1,0:T(8,128)(2,1)} %bitcast.21), calls=%async_computation | async-start | bytes 8388608 | tf_op jit(solution)/shard_map/all_to_all | solution.py:21
  62.5 183.8 %reduce-scatter.2.cloned.1.call-start = ((), (), s32[]{:S(2)}) async-start(), calls=%async_computation.3 | async-start | bytes 4456448 | tf_op jit(solution)/shard_map/reduce_scatter | solution.py:34
  123.1 4.9 %copy-start.4 = (f32[640]{0:T(1024)S(1)}, f32[640]{0:T(1024)}, u32[]{:S(2)}) copy-start(f32[640]{0:T(1024)} %param.11) | copy-start | bytes 7684
  123.1 11.3 %slice-start = ((s8[10485760]{0:T(1024)(128)(4,1)}), s8[4194304]{0:T(1024)(128)(4,1)S(1)}, s32[]{:S(2)}) async-start(s8[10485760]{0:T(1024)(128)(4,1)} %bitcast.29), calls=%async_computation.6 | async-start | bytes 8388608
  126.0 2.0 copy-start
  127.9 6.5 %slice-start.1 = ((s8[10485760]{0:T(1024)(128)(4,1)}), s8[4194304]{0:T(1024)(128)(4,1)S(1)}, s32[]{:S(2)}) async-start(s8[10485760]{0:T(1024)(128)(4,1)} %bitcast.29), calls=%async_computation.7 | async-start | bytes 8388608
  127.9 6.5 %slice-start.2 = ((s8[10485760]{0:T(1024)(128)(4,1)}), s8[2097152]{0:T(1024)(128)(4,1)S(1)}, s32[]{:S(2)}) async-start(s8[10485760]{0:T(1024)(128)(4,1)} %bitcast.29), calls=%async_computation.8 | async-start | bytes 4194304
  145.8 66.7 %all-to-all-start.1 = ((bf16[8,256,1024]{2,1,0:T(8,128)(2,1)}), bf16[8,256,1024]{2,1,0:T(8,128)(2,1)}, u32[]{:S(2)}, u32[]{:S(2)}) async-start(bf16[8,256,1024]{2,1,0:T(8,128)(2,1)} %bitcast.22), calls=%async_computation.1 | async-start | bytes 8388608 | tf_op jit(solution)/shard_map/all_to_all | solution.py:22
  215.2 1.9 copy-start.1
  217.1 29.2 %copy-start.2 = (f32[512]{0:T(512)S(1)}, f32[512]{0:T(512)}, u32[]{:S(2)}) copy-start(f32[512]{0:T(512)} %param.13) | copy-start | bytes 6148
Sparse Core Ops, SparseCore 0:
  9.7 39.7 all-gather.4
  51.2 79.7 all-gather.6
  139.5 106.7 reduce-scatter.1
where the time goes:
time: 285 us
  waiting for transfers between devices  186 us (65%)
  blocking collectives  29.7 us (10%)
  local copies, waits for them, and re-layouts  22.8 us (8%)
  matrix products  18.5 us (6%)
  between operations  13.9 us (5%)
  starting transfers between devices  11.6 us (4%)
    all_to_all x1, waiting for transfers between devices, per_device(): lax.all_to_all(cols_g, 'tok', split_axis=0, concat_axis=1, tiled=True)  61.9 us
    all_to_all x1, waiting for transfers between devices, per_device(): lax.all_to_all(cols_x, 'tok', split_axis=0, concat_axis=1, tiled=True)  59.7 us
    all_gather x1, waiting for transfers between devices, per_device(): lax.all_gather(resid[:, None, :], 'feat', axis=1, tiled=True)  40.8 us
    psum x1, blocking collectives, per_device(): error_attr = lax.psum(local_terms, 'feat')  29.7 us
    reduce_scatter x1, waiting for transfers between devices, per_device(): lax.psum_scatter(partial_recon.astype(jnp.bfloat16), 'feat', scatter_dime...  22.1 us
    dot_general x1, matrix products, per_device(): lax.dot_general(rows_g, w_dec, (((1,), (1,)), ((), ())), preferred_elemen...  7.11 us
    all_to_all x1, starting transfers between devices, per_device(): lax.all_to_all(cols_x, 'tok', split_axis=0, concat_axis=1, tiled=True)  6.65 us
    dot_general x1, matrix products, per_device(): pre = jnp.dot(rows_x, w_enc, preferred_element_type=jnp.float32) + b_enc  6.46 us
  transfers between devices with their start and end apart: 5, of which 4 were waited for; matrix products, arithmetic and copies ran while one was open for 13% of the time, Pallas kernels for 0%

commit v1 on v0

--- a/solution.py
+++ b/solution.py
@@ -12,7 +12,12 @@
     width = resid.shape[1]
     cols_x, cols_g = (
         lax.all_gather(resid[:, None, :], "feat", axis=1, tiled=True),
-        lax.all_gather(resid_grad[:, None, :], "feat", axis=1, tiled=True),
+        jnp.concatenate(
+            lax.all_to_all(
+                jnp.stack([resid_grad[:, None, :]] * lax.axis_size("feat")), "feat", 0, 0
+            ),
+            axis=1,
+        ),
     )
     total = cols_x.shape[0]
     cols_x = cols_x.reshape(total, n_feat * width)

time: 285 us -> 321 us (1.13)
  waiting for transfers between devices: 186 us -> 214 us
  starting transfers between devices: 11.6 us -> 16.3 us
    all_to_all x0 -> x1, waiting for transfers between devices: none -> 38.3 us  [per_device(): lax.all_to_all(jnp.stack([resid_grad[:, None, :]] * lax.axis_size('feat')...]
    reduce_scatter x1, waiting for transfers between devices: 22.1 us -> 8.23 us  [per_device(): lax.psum_scatter(partial_recon.astype(jnp.bfloat16), 'feat', scatter_dime...]
    all_gather x1 -> x0, local copies, waits for them, and re-layouts: 6.36 us -> none  [per_device(): lax.all_gather(resid_grad[:, None, :], 'feat', axis=1, tiled=True)]
    all_to_all x0 -> x1, starting transfers between devices: none -> 4.57 us  [per_device(): lax.all_to_all(jnp.stack([resid_grad[:, None, :]] * lax.axis_size('feat')...]
    all_to_all x1, waiting for transfers between devices: 61.9 us -> 66.1 us  [per_device(): lax.all_to_all(cols_g, 'tok', split_axis=0, concat_axis=1, tiled=True)]
  transfers between devices with their start and end apart: 5 -> 5, of which waited for: 4 -> 5; matrix products, arithmetic and copies ran while one was open for 13% -> 10% of each run, Pallas kernels for 0% -> 0%
where the time goes in v1:
time: 321 us
  waiting for transfers between devices  214 us (67%)
  blocking collectives  31.1 us (10%)
  local copies, waits for them, and re-layouts  21.8 us (7%)
  matrix products  21.2 us (7%)
  starting transfers between devices  16.3 us (5%)
  between operations  14.2 us (4%)
    all_to_all x1, waiting for transfers between devices, per_device(): lax.all_to_all(cols_g, 'tok', split_axis=0, concat_axis=1, tiled=True)  66.1 us
    all_to_all x1, waiting for transfers between devices, per_device(): lax.all_to_all(cols_x, 'tok', split_axis=0, concat_axis=1, tiled=True)  59.2 us
    all_gather x1, waiting for transfers between devices, per_device(): lax.all_gather(resid[:, None, :], 'feat', axis=1, tiled=True)  41.6 us
    all_to_all x1, waiting for transfers between devices, per_device(): lax.all_to_all(jnp.stack([resid_grad[:, None, :]] * lax.axis_size('feat')...  38.3 us
    psum x1, blocking collectives, per_device(): error_attr = lax.psum(local_terms, 'feat')  31.1 us
    dot_general x1, matrix products, per_device(): lax.dot_general(rows_g, w_dec, (((1,), (1,)), ((), ())), preferred_elemen...  9.72 us
    reduce_scatter x1, waiting for transfers between devices, per_device(): lax.psum_scatter(partial_recon.astype(jnp.bfloat16), 'feat', scatter_dime...  8.23 us
    all_to_all x1, starting transfers between devices, per_device(): lax.all_to_all(cols_x, 'tok', split_axis=0, concat_axis=1, tiled=True)  6.65 us
  transfers between devices with their start and end apart: 5, of which 5 were waited for; matrix products, arithmetic and copies ran while one was open for 10% of the time, Pallas kernels for 0%

profile of v1, /device:TPU:0, one launch (start us, length us, event | category | flops | bytes accessed | tf_op | source)
XLA Modules:
  0.0 320.9 jit_solution(16798643893637895423)
XLA Ops:
  7.2 0.0 all-gather.3.cloned.1.call-start
  7.2 0.7 all-gather.3.cloned.1.call-update
  7.9 41.6 %all-gather.3.cloned.1.call-done = bf16[2048,1024]{0,1:T(8,128)(2,1)} async-done(((bf16[2048,64]{0,1:T(8,128)(2,1)}), bf16[2048,1024]{0,1:T(8,128)(2,1)}) %all-gather.3.cloned.1.call-update) | async-done | bytes 4194320 | tf_op jit(solution)/shard_map/all_gather | solution.py:14
  49.5 6.4 %copy.20 = bf16[2048,1024]{1,0:T(8,128)(2,1)} copy(bf16[2048,1024]{0,1:T(8,128)(2,1)} %all-gather.3.cloned.1.call-done) | data formatting | bytes 8388608 | tf_op jit(solution)/shard_map/all_gather | solution.py:14
  55.9 0.0 copy-start.3
  55.9 0.0 copy-start.1
  55.9 6.6 %all-to-all-start = ((bf16[8,256,1024]{2,1,0:T(8,128)(2,1)}), bf16[8,256,1024]{2,1,0:T(8,128)(2,1)}, u32[]{:S(2)}, u32[]{:S(2)}) async-start(bf16[8,256,1024]{2,1,0:T(8,128)(2,1)} %bitcast.27), calls=%async_computation | async-start | bytes 8388608 | tf_op jit(solution)/shard_map/all_to_all | solution.py:26
  62.5 0.0 copy-done.3
  62.5 0.2 compare_reduce_fusion
  62.7 0.1 copy.22
  62.8 0.2 mul.24
  63.1 0.2 copy.23
  63.4 59.2 %all-to-all-done = bf16[8,256,1024]{2,1,0:T(8,128)(2,1)} async-done(((bf16[8,256,1024]{2,1,0:T(8,128)(2,1)}), bf16[8,256,1024]{2,1,0:T(8,128)(2,1)}, u32[]{:S(2)}, u32[]{:S(2)}) %all-to-all-start) | async-done | bytes 4194336 | tf_op jit(solution)/shard_map/all_to_all | solution.py:26
  122.5 0.0 copy-done.1
  122.5 2.4 stack.3
  125.0 4.6 %all-to-all-start.1 = ((bf16[16,2048,1,64]{1,3,2,0:T(8,128)(2,1)}), bf16[16,2048,1,64]{1,3,2,0:T(8,128)(2,1)}, u32[]{:S(2)}, u32[]{:S(2)}) async-start(bf16[16,2048,1,64]{1,3,2,0:T(8,128)(2,1)} %stack.3), calls=%async_computation.1 | async-start | bytes 8388608 | tf_op jit(solution)/shard_map/all_to_all | solution.py:16
  129.6 0.0 reduce-scatter.2.cloned.1.call-start
  129.6 0.0 copy-start.4
  129.6 0.0 slice-start
  129.6 2.8 copy.28
  132.4 0.0 copy-start
  132.5 1.9 copy-done
  134.4 0.0 copy-done.4
  134.4 0.0 slice-start.1
  134.4 0.0 slice-start.2
  134.4 6.4 %fusion.2 = bf16[256,640]{1,0:T(8,128)(2,1)S(1)} fusion(f32[256,640]{1,0:T(8,128)S(1)} %copy.23, bf16[256,8192]{1,0:T(8,128)(2,1)S(1)} %bitcast.29, bf16[8192,640]{1,0:T(8,128)(2,1)} %param.10, f32[640]{0:T(1024)S(1)} %copy-done.4), kind=kOutput, calls=%fused_computation.5 | convolution fusion | flops 2685009920 | bytes 15665664 | tf_op jit(solution)/shard_map/dot_general | solution.py:35
  140.8 0.0 slice-done
  140.9 0.0 slice-done.1
  140.9 0.0 slice-done.2
  140.9 5.1 %convolution_convert_fusion = bf16[256,8192]{1,0:T(8,128)(2,1)} fusion(bf16[256,640]{1,0:T(8,128)(2,1)S(1)} %fusion.2, bf16[640,8192]{1,0:T(8,128)(2,1)S(1)} %bitcast.34), kind=kOutput, calls=%fused_computation | convolution fusion | flops 2686451712 | bytes 15007744 | tf_op jit(solution)/shard_map/dot_general | solution.py:38
  145.9 0.0 reduce-scatter.2.cloned.1.call-update
  146.0 38.3 %all-to-all-done.1 = bf16[16,2048,1,64]{1,3,2,0:T(8,128)(2,1)} async-done(((bf16[16,2048,1,64]{1,3,2,0:T(8,128)(2,1)}), bf16[16,2048,1,64]{1,3,2,0:T(8,128)(2,1)}, u32[]{:S(2)}, u32[]{:S(2)}) %all-to-all-start.1) | async-done | bytes 4194336 | tf_op jit(solution)/shard_map/all_to_all | solution.py:16
  184.3 3.7 %copy.30 = bf16[128,8,8,256]{3,2,1,0:T(8,128)(2,1)S(1)} copy(bf16[128,8,8,256]{3,1,2,0:T(8,128)(2,1)} %bitcast.16) | data formatting | bytes 8388608
  188.0 2.8 copy.24
  190.8 5.0 %all-to-all-start.2 = ((bf16[8,256,1024]{1,2,0:T(8,128)(2,1)}), bf16[8,256,1024]{1,2,0:T(8,128)(2,1)}, u32[]{:S(2)}, u32[]{:S(2)}) async-start(bf16[8,256,1024]{1,2,0:T(8,128)(2,1)} %copy.24), calls=%async_computation.2 | async-start | bytes 8388608 | tf_op jit(solution)/shard_map/all_to_all | solution.py:27
  195.8 66.1 %all-to-all-done.2 = bf16[8,256,1024]{1,2,0:T(8,128)(2,1)} async-done(((bf16[8,256,1024]{1,2,0:T(8,128)(2,1)}), bf16[8,256,1024]{1,2,0:T(8,128)(2,1)}, u32[]{:S(2)}, u32[]{:S(2)}) %all-to-all-start.2) | async-done | bytes 4194336 | tf_op jit(solution)/shard_map/all_to_all | solution.py:27
  261.9 1.0 constant_dynamic-slice_fusion
  262.9 0.1 copy.27
  263.0 0.0 copy-start.2
  263.0 9.7 %convolution_multiply_fusion = f32[256,640]{1,0:T(8,128)} fusion(bf16[256,8192]{0,1:T(8,128)(2,1)} %bitcast.4, bf16[640,8192]{1,0:T(8,128)(2,1)} %param.12, bf16[256,640]{1,0:T(8,128)(2,1)S(1)} %fusion.2), kind=kOutput, calls=%fused_computation.1 | convolution fusion | flops 2684682240 | bytes 15663104 | tf_op jit(solution)/shard_map/dot_general | solution.py:50
  272.7 8.2 %reduce-scatter.2.cloned.1.call-done = bf16[256,512]{1,0:T(8,128)(2,1)} async-done(((bf16[256,8192]{1,0:T(8,128)(2,1)}), bf16[256,512]{1,0:T(8,128)(2,1)}) %reduce-scatter.2.cloned.1.call-update) | async-done | bytes 262160 | tf_op jit(solution)/shard_map/reduce_scatter | solution.py:39
  281.0 0.0 copy-done.2
  281.0 1.9 multiply_reduce_fusion
  282.9 31.1 %psum.7 = f32[256]{0:T(256)} all-reduce(f32[256]{0:T(256)S(1)} %get-tuple-element.3), channel_id=1, replica_groups=mesh['tok'=8,'feat'=16] {'feat'}, use_global_device_ids=true, to_apply=%region_3.0 | all-reduce | flops 256 | bytes 2048 | tf_op jit(solution)/shard_map/psum | solution.py:49
  (4 shorter events, 0.1 us)
Async XLA Ops:
  7.2 42.3 %all-gather.3.cloned.1.call-start = ((), (), s32[]{:S(2)}) async-start(), calls=%async_computation.5 | async-start | bytes 4456448 | tf_op jit(solution)/shard_map/all_gather | solution.py:14
  55.9 6.7 %copy-start.3 = (s32[2,20]{1,0:T(2,128)S(1)}, s32[2,20]{1,0:T(2,128)}, u32[]{:S(2)}) copy-start(s32[2,20]{1,0:T(2,128)} %param.9) | copy-start | bytes 484
  55.9 66.7 %copy-start.1 = (bf16[2048,64]{0,1:T(8,128)(2,1)S(1)}, bf16[2048,64]{0,1:T(8,128)(2,1)}, u32[]{:S(2)}) copy-start(bf16[2048,64]{0,1:T(8,128)(2,1)} %param.8) | copy-start | bytes 786436
  55.9 66.6 %all-to-all-start = ((bf16[8,256,1024]{2,1,0:T(8,128)(2,1)}), bf16[8,256,1024]{2,1,0:T(8,128)(2,1)}, u32[]{:S(2)}, u32[]{:S(2)}) async-start(bf16[8,256,1024]{2,1,0:T(8,128)(2,1)} %bitcast.27), calls=%async_computation | async-start | bytes 8388608 | tf_op jit(solution)/shard_map/all_to_all | solution.py:26
  125.0 59.3 %all-to-all-start.1 = ((bf16[16,2048,1,64]{1,3,2,0:T(8,128)(2,1)}), bf16[16,2048,1,64]{1,3,2,0:T(8,128)(2,1)}, u32[]{:S(2)}, u32[]{:S(2)}) async-start(bf16[16,2048,1,64]{1,3,2,0:T(8,128)(2,1)} %stack.3), calls=%async_computation.1 | async-start | bytes 8388608 | tf_op jit(solution)/shard_map/all_to_all | solution.py:16
  129.6 151.4 %reduce-scatter.2.cloned.1.call-start = ((), (), s32[]{:S(2)}) async-start(), calls=%async_computation.4 | async-start | bytes 4456448 | tf_op jit(solution)/shard_map/reduce_scatter | solution.py:39
  129.6 4.8 %copy-start.4 = (f32[640]{0:T(1024)S(1)}, f32[640]{0:T(1024)}, u32[]{:S(2)}) copy-start(f32[640]{0:T(1024)} %param.11) | copy-start | bytes 7684
  129.6 11.2 %slice-start = ((s8[10485760]{0:T(1024)(128)(4,1)}), s8[4194304]{0:T(1024)(128)(4,1)S(1)}, s32[]{:S(2)}) async-start(s8[10485760]{0:T(1024)(128)(4,1)} %bitcast.33), calls=%async_computation.6 | async-start | bytes 8388608
  132.4 2.0 copy-start
  134.4 6.5 %slice-start.1 = ((s8[10485760]{0:T(1024)(128)(4,1)}), s8[4194304]{0:T(1024)(128)(4,1)S(1)}, s32[]{:S(2)}) async-start(s8[10485760]{0:T(1024)(128)(4,1)} %bitcast.33), calls=%async_computation.7 | async-start | bytes 8388608
  134.4 6.5 %slice-start.2 = ((s8[10485760]{0:T(1024)(128)(4,1)}), s8[2097152]{0:T(1024)(128)(4,1)S(1)}, s32[]{:S(2)}) async-start(s8[10485760]{0:T(1024)(128)(4,1)} %bitcast.33), calls=%async_computation.8 | async-start | bytes 4194304
  190.8 71.1 %all-to-all-start.2 = ((bf16[8,256,1024]{1,2,0:T(8,128)(2,1)}), bf16[8,256,1024]{1,2,0:T(8,128)(2,1)}, u32[]{:S(2)}, u32[]{:S(2)}) async-start(bf16[8,256,1024]{1,2,0:T(8,128)(2,1)} %copy.24), calls=%async_computation.2 | async-start | bytes 8388608 | tf_op jit(solution)/shard_map/all_to_all | solution.py:27
  263.0 18.0 %copy-start.2 = (f32[512]{0:T(512)S(1)}, f32[512]{0:T(512)}, u32[]{:S(2)}) copy-start(f32[512]{0:T(512)} %param.13) | copy-start | bytes 6148
Sparse Core Ops, SparseCore 0:
  9.7 39.7 all-gather.2
  146.1 134.8 reduce-scatter.1
